TPU v7x, 512 devices: a whole 4x8x8 slice. The times are simulated.
512 devices in a mesh: seq: 128 (over x, z, y_hi), tp: 4 (over y_lo, core).
Axes of the slice: x: 4, y: 8 (y_hi: 4, y_lo: 2; y = y_hi * 2 + y_lo), z: 8, core: 2. Of those that a mesh axis runs over, the one named last changes fastest.
Arguments:
- residual_in: float32 [32768, 2048], P('seq', 'tp'), may hold values from -18 to 18
- query_rows: bfloat16 [32768, 2048], P('seq', 'tp'), may hold values from -6 to 6
- key_rows: bfloat16 [32768, 2048], P('seq', 'tp'), may hold values from -6 to 6
- value_rows: bfloat16 [32768, 2048], P('seq', 'tp'), may hold values from -6 to 6
- lengths: int32 [256], P('seq'), may hold values from 0 to 128, as said below
- norm_gain: float32 [2048], P('tp'), may hold values from 0.1 to 1.9
- gate_weight: bfloat16 [2048, 4096], P('seq', 'tp'), may hold values from -0.125 to 0.125
- up_weight: bfloat16 [2048, 4096], P('seq', 'tp'), may hold values from -0.125 to 0.125
- down_weight: bfloat16 [4096, 2048], P('tp', 'seq'), may hold values from -0.375 to 0.375
Outputs:
- attended: bfloat16 [32768, 2048], P('seq', 'tp')
- mixed: float32 [32768, 2048], P('seq', 'tp')
Inputs may be any that keep to these rules, and one draw needn't show every extreme that they name: `lengths`: entry s counts the valid events at the start of segment s, the events s * 128 to s * 128 + 127; the rest of the segment is padding.
All inputs are finite; a program needn't handle non-finite values.
Results may differ from a plain program's by a relative error of at most 0.008.
Values may be sent and summed in bfloat16 or wider, within the bound.
No kernel may reach another device: no remote copies, remote signals or barrier semaphores. Data moves between devices by JAX's collectives and lax.ppermute only.
A program may use at most 64 MiB of HBM per device.

v0:
```python
import math
import jax
import jax.numpy as jnp
from jax import lax
from jax.sharding import PartitionSpec as P

D = 2048
HEAD_DIM = 128
SEG = 128
WINDOW = 512
epsilon = 1e-06


def from_behind(value, axis, by):
    size = lax.axis_size(axis)
    pairs = [(i, i + by) for i in range(size) if 0 <= i + by < size]
    return lax.ppermute(value, axis, pairs)


def on_device(
    residual_in,
    query_rows,
    key_rows,
    value_rows,
    lengths,
    norm_gain,
    gate_weight,
    up_weight,
    down_weight,
):
    row_count = query_rows.shape[0]
    head_local = query_rows.shape[1] // HEAD_DIM
    reach_blocks = (WINDOW + row_count - 2) // row_count
    seq_index = lax.axis_index("seq")
    offsets = jnp.arange(row_count, dtype=jnp.int32) % SEG
    own_valid = (offsets < jnp.repeat(lengths, SEG, total_repeat_length=row_count)).astype(
        jnp.bfloat16
    )
    previous = from_behind((key_rows, value_rows, own_valid), "seq", 1)
    earlier = [previous]
    earlier.append(from_behind((key_rows, value_rows, own_valid), "seq", 2))
    oldest_first = earlier[::-1]
    key_window = jnp.concatenate([block[0] for block in oldest_first] + [key_rows], axis=0)
    value_window = jnp.concatenate([block[1] for block in oldest_first] + [value_rows], axis=0)
    valid_window = jnp.concatenate([block[2] for block in oldest_first] + [own_valid], axis=0)
    key_span = key_window.shape[0]
    query_pos = seq_index * row_count + jnp.arange(row_count, dtype=jnp.int32)
    key_pos = (seq_index - reach_blocks) * row_count + jnp.arange(key_span, dtype=jnp.int32)
    allowed = (key_pos[None, :] <= query_pos[:, None]) & (
        key_pos[None, :] > query_pos[:, None] - WINDOW
    )
    allowed = allowed & (key_pos[None, :] >= 0) & (valid_window[None, :] > 0)
    keep_rows = (own_valid > 0)[:, None]
    score_scale = 1.0 / math.sqrt(HEAD_DIM)
    outputs = []
    for head_index in range(head_local):
        low_col = head_index * HEAD_DIM
        query_head = query_rows[:, low_col : low_col + HEAD_DIM]
        key_head = key_window[:, low_col : low_col + HEAD_DIM]
        value_head = value_window[:, low_col : low_col + HEAD_DIM]
        scores = (
            lax.dot_general(
                query_head, key_head, (((1,), (1,)), ((), ())), preferred_element_type=jnp.float32
            )
            * score_scale
        )
        masked = jnp.where(allowed, scores, -1e30)
        row_max = jnp.max(masked, axis=1, keepdims=True)
        weights = jnp.where(allowed, jnp.exp(masked - row_max), 0.0)
        denominator = jnp.sum(weights, axis=1, keepdims=True)
        numerator = jnp.dot(
            weights.astype(jnp.bfloat16), value_head, preferred_element_type=jnp.float32
        )
        outputs.append(
            jnp.where(keep_rows, numerator / jnp.where(keep_rows, denominator, 1.0), 0.0)
        )
    attended = jnp.concatenate(outputs, axis=1).astype(jnp.bfloat16)
    residual = residual_in + attended.astype(jnp.float32)
    square_sum = lax.psum(jnp.sum(residual * residual, axis=1), "tp")
    inverse = lax.rsqrt(square_sum / D + epsilon)
    normed = (residual * inverse[:, None] * norm_gain[None, :]).astype(jnp.bfloat16)
    normed_full = lax.all_gather(normed, "tp", axis=1, tiled=True)
    gate_full, up_full = (
        lax.all_gather(gate_weight, "seq", axis=0, tiled=True),
        lax.all_gather(up_weight, "seq", axis=0, tiled=True),
    )
    gate_sum = jnp.dot(normed_full, gate_full, preferred_element_type=jnp.float32)
    up_sum = jnp.dot(normed_full, up_full, preferred_element_type=jnp.float32)
    hidden = (jax.nn.silu(gate_sum) * up_sum).astype(jnp.bfloat16)
    down_full = lax.all_gather(down_weight, "seq", axis=1, tiled=True)
    partial_value = jnp.dot(hidden, down_full, preferred_element_type=jnp.float32)
    tp_width = residual_in.shape[1]
    summed = lax.psum(partial_value.astype(jnp.bfloat16), "tp").astype(jnp.float32)
    branch_share = lax.dynamic_slice_in_dim(summed, lax.axis_index("tp") * tp_width, tp_width, 1)
    mixed = residual + branch_share
    return (attended, mixed)


def solution(mesh):
    placed = (
        P("seq", "tp"),
        P("seq", "tp"),
        P("seq", "tp"),
        P("seq", "tp"),
        P("seq"),
        P("tp"),
        P("seq", "tp"),
        P("seq", "tp"),
        P("tp", "seq"),
    )
    return jax.shard_map(
        on_device,
        mesh=mesh,
        in_specs=placed,
        out_specs=(P("seq", "tp"), P("seq", "tp")),
        check_vma=False,
    )
```

profile of v0, /device:TPU:1, one launch (start us, length us, event | category | flops | bytes accessed | tf_op | source)
XLA Modules:
  0.0 574.4 jit_solution(10562217400988549649)
XLA Ops:
  7.2 1.3 fusion.57
  8.6 1.3 compare_select_fusion.1
  9.9 8.3 %collective-permute-start = (bf16[256]{0:T(256)(128)(2,1)S(1)}, bf16[256]{0:T(256)(128)(2,1)S(1)}, u32[]{:S(2)}, u32[]{:S(2)}) collective-permute-start(bf16[256]{0:T(256)(128)(2,1)S(1)} %get-tuple-element.21), channel_id=1, source_target_pairs={{0,8},{4,12},{8,16},{12,20},{16,24},{20,28},{24,32},{28,36},{32,40... | collective-permute-start | bytes 1544 | tf_op jit(solution)/shard_map/ppermute | solution.py:17
  18.2 2.4 collective-permute-start.1
  20.6 5.4 collective-permute-start.2
  26.0 5.4 collective-permute-start.3
  31.4 3.5 collective-permute-start.4
  35.0 1.2 copy.11
  36.3 4.2 collective-permute-start.5
  40.6 2.4 collective-permute-done.3
  43.9 1.3 fusion.59
  46.1 3.1 collective-permute-done.4
  49.6 10.2 %collective-permute-done.5 = bf16[256,512]{1,0:T(8,128)(2,1)S(1)} collective-permute-done((bf16[256,512]{1,0:T(8,128)(2,1)}, bf16[256,512]{1,0:T(8,128)(2,1)S(1)}, u32[]{:S(2)}, u32[]{:S(2)}) %collective-permute-start.5) | collective-permute-done | bytes 262176 | tf_op jit(solution)/shard_map/ppermute | solution.py:17
  59.8 1.0 fusion.17
  63.5 17.3 %psum.14 = f32[256]{0:T(256)S(1)} all-reduce(f32[256]{0:T(256)S(1)} %multiply_reduce_fusion), channel_id=1, replica_groups=mesh['seq'=128,'tp'=4] {'tp'}, use_global_device_ids=true, to_apply=%region_9.10 | all-reduce | flops 256 | bytes 2048 | tf_op jit(solution)/shard_map/psum | solution.py:79
  83.7 29.9 %all-gather.5.cloned.1.call-done = bf16[256,2048]{0,1:T(8,128)(2,1)} async-done(((bf16[256,512]{0,1:T(8,128)(2,1)}), bf16[256,2048]{0,1:T(8,128)(2,1)}) %all-gather.5.cloned.1.call-update) | async-done | bytes 1048592 | tf_op jit(solution)/shard_map/all_gather | solution.py:82
  113.7 132.3 %all-gather.7.cloned.1.call-done = bf16[2048,1024]{1,0:T(8,128)(2,1)} async-done(((bf16[16,1024]{1,0:T(8,128)(2,1)}), bf16[2048,1024]{1,0:T(8,128)(2,1)}) %all-gather.7.cloned.1.call-update) | async-done | bytes 4194320 | tf_op jit(solution)/shard_map/all_gather | solution.py:84
  245.9 3.8 fusion.62
  249.7 127.1 %all-gather.11.cloned.1.call-done = bf16[1024,2048]{0,1:T(8,128)(2,1)} async-done(((bf16[1024,16]{0,1:T(8,128)(2,1)}), bf16[1024,2048]{0,1:T(8,128)(2,1)}) %all-gather.11.cloned.1.call-update) | async-done | bytes 4194320 | tf_op jit(solution)/shard_map/all_gather | solution.py:90
  376.8 130.7 %all-gather.9.cloned.1.call-done = bf16[2048,1024]{1,0:T(8,128)(2,1)} async-done(((bf16[16,1024]{1,0:T(8,128)(2,1)}), bf16[2048,1024]{1,0:T(8,128)(2,1)}) %all-gather.9.cloned.1.call-update) | async-done | bytes 4194320 | tf_op jit(solution)/shard_map/all_gather | solution.py:85
  507.5 7.1 %convolution_convert_fusion = bf16[256,2048]{0,1:T(8,128)(2,1)} fusion(bf16[1024,2048]{0,1:T(8,128)(2,1)} %all-gather.11.cloned.1.call-done, bf16[256,2048]{0,1:T(8,128)(2,1)S(1)} %copy-done.2, bf16[2048,1024]{1,0:T(8,128)(2,1)} %all-gather.9.cloned.1.call-done, f32[256,1024]{1,0:T(8,128)S(1)} %fusion.62), kind=kOutput, calls=%fused_computation | convolution fusion | flops 2149580800 | bytes 11534336 | tf_op jit(solution)/shard_map/dot_general | solution.py:91
  515.5 50.4 %all-reduce.2.cloned.1.call-done = bf16[256,2048]{0,1:T(8,128)(2,1)} async-done(((bf16[256,2048]{0,1:T(8,128)(2,1)}), bf16[256,2048]{0,1:T(8,128)(2,1)}) %all-reduce.2.cloned.1.call-update) | async-done | bytes 1048592 | tf_op jit(solution)/shard_map/psum | solution.py:93
  565.9 1.0 convert_add_fusion
  566.9 1.0 copy.14
  (47 shorter events, 8.8 us)
Async XLA Ops:
  7.2 38.1 %copy-start.3 = (bf16[256,512]{1,0:T(8,128)(2,1)S(1)}, bf16[256,512]{1,0:T(8,128)(2,1)}, u32[]{:S(2)}) copy-start(bf16[256,512]{1,0:T(8,128)(2,1)} %param.12) | copy-start | bytes 786436
  7.2 106.5 %all-gather.5.cloned.1.call-start = ((), (), s32[]{:S(2)}) async-start(), calls=%async_computation | async-start | bytes 1310720 | tf_op jit(solution)/shard_map/all_gather | solution.py:82
  9.9 26.4 %collective-permute-start = (bf16[256]{0:T(256)(128)(2,1)S(1)}, bf16[256]{0:T(256)(128)(2,1)S(1)}, u32[]{:S(2)}, u32[]{:S(2)}) collective-permute-start(bf16[256]{0:T(256)(128)(2,1)S(1)} %get-tuple-element.21), channel_id=1, source_target_pairs={{0,8},{4,12},{8,16},{12,20},{16,24},{20,28},{24,32},{28,36},{32,40... | collective-permute-start | bytes 1544 | tf_op jit(solution)/shard_map/ppermute | solution.py:17
  18.2 22.3 %collective-permute-start.1 = (bf16[256]{0:T(256)(128)(2,1)S(1)}, bf16[256]{0:T(256)(128)(2,1)S(1)}, u32[]{:S(2)}, u32[]{:S(2)}) collective-permute-start(bf16[256]{0:T(256)(128)(2,1)S(1)} %get-tuple-element.21), channel_id=1, source_target_pairs={{0,4},{4,8},{8,12},{12,16},{16,20},{20,24},{24,28},{28,32},{32,36}... | collective-permute-start | bytes 1544 | tf_op jit(solution)/shard_map/ppermute | solution.py:17
  20.6 19.9 %collective-permute-start.2 = (bf16[256,512]{1,0:T(8,128)(2,1)}, bf16[256,512]{1,0:T(8,128)(2,1)S(1)}, u32[]{:S(2)}, u32[]{:S(2)}) collective-permute-start(bf16[256,512]{1,0:T(8,128)(2,1)} %param.13), channel_id=1, source_target_pairs={{0,8},{4,12},{8,16},{12,20},{16,24},{20,28},{24,32},{28,36},{32,40... | collective-permute-start | bytes 786440 | tf_op jit(solution)/shard_map/ppermute | solution.py:17
  26.0 17.0 %collective-permute-start.3 = (bf16[256,512]{1,0:T(8,128)(2,1)}, bf16[256,512]{1,0:T(8,128)(2,1)S(1)}, u32[]{:S(2)}, u32[]{:S(2)}) collective-permute-start(bf16[256,512]{1,0:T(8,128)(2,1)} %param.13), channel_id=1, source_target_pairs={{0,4},{4,8},{8,12},{12,16},{16,20},{20,24},{24,28},{28,32},{32,36}... | collective-permute-start | bytes 786440 | tf_op jit(solution)/shard_map/ppermute | solution.py:17
  31.4 17.8 %collective-permute-start.4 = (bf16[256,512]{1,0:T(8,128)(2,1)}, bf16[256,512]{1,0:T(8,128)(2,1)S(1)}, u32[]{:S(2)}, u32[]{:S(2)}) collective-permute-start(bf16[256,512]{1,0:T(8,128)(2,1)} %param.14), channel_id=1, source_target_pairs={{0,8},{4,12},{8,16},{12,20},{16,24},{20,28},{24,32},{28,36},{32,40... | collective-permute-start | bytes 786440 | tf_op jit(solution)/shard_map/ppermute | solution.py:17
  36.3 23.5 %collective-permute-start.5 = (bf16[256,512]{1,0:T(8,128)(2,1)}, bf16[256,512]{1,0:T(8,128)(2,1)S(1)}, u32[]{:S(2)}, u32[]{:S(2)}) collective-permute-start(bf16[256,512]{1,0:T(8,128)(2,1)} %param.14), channel_id=1, source_target_pairs={{0,4},{4,8},{8,12},{12,16},{16,20},{20,24},{24,28},{28,32},{32,36}... | collective-permute-start | bytes 786440 | tf_op jit(solution)/shard_map/ppermute | solution.py:17
  43.9 15.9 %copy-start = (bf16[256,512]{1,0:T(8,128)(2,1)S(1)}, bf16[256,512]{1,0:T(8,128)(2,1)}, u32[]{:S(2)}) copy-start(bf16[256,512]{1,0:T(8,128)(2,1)} %param.14) | copy-start | bytes 786436
  61.5 19.2 %copy-start.1 = (f32[512]{0:T(512)S(1)}, f32[512]{0:T(512)}, u32[]{:S(2)}) copy-start(f32[512]{0:T(512)} %param.16) | copy-start | bytes 6148
  81.6 164.3 %all-gather.7.cloned.1.call-start = ((), (), s32[]{:S(2)}) async-start(), calls=%async_computation.1 | async-start | bytes 4227072 | tf_op jit(solution)/shard_map/all_gather | solution.py:84
  82.4 294.4 %all-gather.11.cloned.1.call-start = ((), (), s32[]{:S(2)}) async-start(), calls=%async_computation.3 | async-start | bytes 4227072 | tf_op jit(solution)/shard_map/all_gather | solution.py:90
  83.1 424.4 %all-gather.9.cloned.1.call-start = ((), (), s32[]{:S(2)}) async-start(), calls=%async_computation.2 | async-start | bytes 4227072 | tf_op jit(solution)/shard_map/all_gather | solution.py:85
  83.7 482.2 %all-reduce.2.cloned.1.call-start = ((), (), s32[]{:S(2)}) async-start(), calls=%async_computation.4 | async-start | bytes 2097152 | tf_op jit(solution)/shard_map/psum | solution.py:93
  113.7 393.9 %copy-start.2 = (bf16[256,2048]{0,1:T(8,128)(2,1)S(1)}, bf16[256,2048]{0,1:T(8,128)(2,1)}, u32[]{:S(2)}) copy-start(bf16[256,2048]{0,1:T(8,128)(2,1)} %all-gather.5.cloned.1.call-done) | copy-start | bytes 3145732
Sparse Core Ops, SparseCore 0:
  81.7 31.8 all-gather.4
  118.2 127.7 all-gather.6
  250.5 126.2 all-gather.10
  381.2 126.2 all-gather.8
  514.7 51.0 all-reduce.1
where the time goes:
time: 575 us; the launch traced here: 574 us
  waiting for transfers between devices  488 us (85%)
  starting transfers between devices  29.5 us (5%)
  blocking collectives  17.3 us (3%)
  matrix products  15.9 us (3%)
  between operations  14.1 us (2%)
    all_gather x1, waiting for transfers between devices, on_device(): lax.all_gather(gate_weight, 'seq', axis=0, tiled=True)  132 us
    all_gather x1, waiting for transfers between devices, on_device(): lax.all_gather(up_weight, 'seq', axis=0, tiled=True)  131 us
    all_gather x1, waiting for transfers between devices, on_device(): down_full = lax.all_gather(down_weight, 'seq', axis=1, tiled=True)  127 us
    psum x1, waiting for transfers between devices, on_device(): lax.psum(partial_value.astype(jnp.bfloat16), 'tp').astype(jnp.float32)  50.4 us
    all_gather x1, waiting for transfers between devices, on_device(): normed_full = lax.all_gather(normed, 'tp', axis=1, tiled=True)  29.9 us
    ppermute x6, starting transfers between devices, from_behind(): return lax.ppermute(value, axis, pairs)  29.3 us
    psum x1, blocking collectives, on_device(): square_sum = lax.psum(jnp.sum(residual * residual, axis=1), 'tp')  17.3 us
    ppermute x6, waiting for transfers between devices, from_behind(): return lax.ppermute(value, axis, pairs)  15.6 us
  transfers between devices with their start and end apart: 11, of which 8 were waited for; matrix products, arithmetic and copies ran while one was open for 2% of the time, Pallas kernels for 0%

commit v1 on v0

--- a/solution.py
+++ b/solution.py
@@ -87,7 +87,10 @@
     gate_sum = jnp.dot(normed_full, gate_full, preferred_element_type=jnp.float32)
     up_sum = jnp.dot(normed_full, up_full, preferred_element_type=jnp.float32)
     hidden = (jax.nn.silu(gate_sum) * up_sum).astype(jnp.bfloat16)
-    down_full = lax.all_gather(down_weight, "seq", axis=1, tiled=True)
+    peers = lax.axis_size("seq")
+    pieces = jnp.stack([down_weight for _ in range(peers)])
+    pieces = lax.all_to_all(pieces, "seq", split_axis=0, concat_axis=0)
+    down_full = jnp.concatenate(pieces, axis=1)
     partial_value = jnp.dot(hidden, down_full, preferred_element_type=jnp.float32)
     tp_width = residual_in.shape[1]
     summed = lax.psum(partial_value.astype(jnp.bfloat16), "tp").astype(jnp.float32)

time: 575 us -> 507 us (0.88)
  waiting for transfers between devices: 488 us -> 397 us
  starting transfers between devices: 29.5 us -> 49.4 us
    all_gather x1 -> x0, waiting for transfers between devices: 127 us -> none  [on_device(): down_full = lax.all_gather(down_weight, 'seq', axis=1, tiled=True)]
    all_gather x1, waiting for transfers between devices: 132 us -> 162 us  [on_device(): lax.all_gather(gate_weight, 'seq', axis=0, tiled=True)]
    all_to_all x0 -> x1, starting transfers between devices: none -> 20 us  [on_device(): pieces = lax.all_to_all(pieces, 'seq', split_axis=0, concat_axis=0)]
    all_gather x1, waiting for transfers between devices: 29.9 us -> 40.4 us  [on_device(): normed_full = lax.all_gather(normed, 'tp', axis=1, tiled=True)]
  transfers between devices with their start and end apart: 11 -> 11, of which waited for: 8 -> 7; matrix products, arithmetic and copies ran while one was open for 2% -> 2% of each run, Pallas kernels for 0% -> 0%
where the time goes in v1:
time: 507 us; the launch traced here: 506 us
  waiting for transfers between devices  397 us (78%)
  starting transfers between devices  49.4 us (10%)
  blocking collectives  17.3 us (3%)
  matrix products  15.9 us (3%)
  between operations  14.1 us (3%)
  local copies, waits for them, and re-layouts  7.97 us (2%)
    all_gather x1, waiting for transfers between devices, on_device(): lax.all_gather(gate_weight, 'seq', axis=0, tiled=True)  162 us
    all_gather x1, waiting for transfers between devices, on_device(): lax.all_gather(up_weight, 'seq', axis=0, tiled=True)  127 us
    psum x1, waiting for transfers between devices, on_device(): lax.psum(partial_value.astype(jnp.bfloat16), 'tp').astype(jnp.float32)  50.4 us
    all_gather x1, waiting for transfers between devices, on_device(): normed_full = lax.all_gather(normed, 'tp', axis=1, tiled=True)  40.4 us
    ppermute x6, starting transfers between devices, from_behind(): return lax.ppermute(value, axis, pairs)  29.3 us
    all_to_all x1, starting transfers between devices, on_device(): pieces = lax.all_to_all(pieces, 'seq', split_axis=0, concat_axis=0)  20 us
    psum x1, blocking collectives, on_device(): square_sum = lax.psum(jnp.sum(residual * residual, axis=1), 'tp')  17.3 us
    ppermute x6, waiting for transfers between devices, from_behind(): return lax.ppermute(value, axis, pairs)  15.6 us
  transfers between devices with their start and end apart: 11, of which 7 were waited for; matrix products, arithmetic and copies ran while one was open for 2% of the time, Pallas kernels for 0%

profile of v1, /device:TPU:1, one launch (start us, length us, event | category | flops | bytes accessed | tf_op | source)
XLA Modules:
  0.0 506.1 jit_solution(1237730198919685634)
XLA Ops:
  7.2 1.3 fusion.57
  8.6 1.3 compare_select_fusion.1
  9.9 8.3 %collective-permute-start = (bf16[256]{0:T(256)(128)(2,1)S(1)}, bf16[256]{0:T(256)(128)(2,1)S(1)}, u32[]{:S(2)}, u32[]{:S(2)}) collective-permute-start(bf16[256]{0:T(256)(128)(2,1)S(1)} %get-tuple-element.23), channel_id=1, source_target_pairs={{0,8},{4,12},{8,16},{12,20},{16,24},{20,28},{24,32},{28,36},{32,40... | collective-permute-start | bytes 1544 | tf_op jit(solution)/shard_map/ppermute | solution.py:17
  18.2 2.4 collective-permute-start.1
  20.6 5.4 %collective-permute-start.2 = (bf16[256,512]{1,0:T(8,128)(2,1)}, bf16[256,512]{1,0:T(8,128)(2,1)S(1)}, u32[]{:S(2)}, u32[]{:S(2)}) collective-permute-start(bf16[256,512]{1,0:T(8,128)(2,1)} %param.13), channel_id=1, source_target_pairs={{0,8},{4,12},{8,16},{12,20},{16,24},{20,28},{24,32},{28,36},{32,40... | collective-permute-start | bytes 786440 | tf_op jit(solution)/shard_map/ppermute | solution.py:17
  26.0 5.4 %collective-permute-start.3 = (bf16[256,512]{1,0:T(8,128)(2,1)}, bf16[256,512]{1,0:T(8,128)(2,1)S(1)}, u32[]{:S(2)}, u32[]{:S(2)}) collective-permute-start(bf16[256,512]{1,0:T(8,128)(2,1)} %param.13), channel_id=1, source_target_pairs={{0,4},{4,8},{8,12},{12,16},{16,20},{20,24},{24,28},{28,32},{32,36}... | collective-permute-start | bytes 786440 | tf_op jit(solution)/shard_map/ppermute | solution.py:17
  31.4 3.5 collective-permute-start.4
  35.0 1.2 copy.16
  36.3 4.2 collective-permute-start.5
  40.6 2.4 collective-permute-done.3
  43.9 1.3 fusion.59
  46.1 3.1 collective-permute-done.4
  49.6 10.2 %collective-permute-done.5 = bf16[256,512]{1,0:T(8,128)(2,1)S(1)} collective-permute-done((bf16[256,512]{1,0:T(8,128)(2,1)}, bf16[256,512]{1,0:T(8,128)(2,1)S(1)}, u32[]{:S(2)}, u32[]{:S(2)}) %collective-permute-start.5) | collective-permute-done | bytes 262176 | tf_op jit(solution)/shard_map/ppermute | solution.py:17
  59.8 1.0 fusion.17
  63.5 17.3 %psum.14 = f32[256]{0:T(256)S(1)} all-reduce(f32[256]{0:T(256)S(1)} %multiply_reduce_fusion), channel_id=1, replica_groups=mesh['seq'=128,'tp'=4] {'tp'}, use_global_device_ids=true, to_apply=%region_9.10 | all-reduce | flops 256 | bytes 2048 | tf_op jit(solution)/shard_map/psum | solution.py:79
  83.1 2.5 stack.2
  85.6 20.0 %all-to-all-start = ((bf16[128,1024,16]{1,2,0:T(8,128)(2,1)}), bf16[128,1024,16]{1,2,0:T(8,128)(2,1)}, u32[]{:S(2)}, u32[]{:S(2)}) async-start(bf16[128,1024,16]{1,2,0:T(8,128)(2,1)} %stack.2), calls=%async_computation | async-start | bytes 8388608 | tf_op jit(solution)/shard_map/all_to_all | solution.py:92
  105.6 40.4 %all-gather.4.cloned.1.call-done = bf16[256,2048]{0,1:T(8,128)(2,1)} async-done(((bf16[256,512]{0,1:T(8,128)(2,1)}), bf16[256,2048]{0,1:T(8,128)(2,1)}) %all-gather.4.cloned.1.call-update) | async-done | bytes 1048592 | tf_op jit(solution)/shard_map/all_gather | solution.py:82
  146.0 162.2 %all-gather.6.cloned.1.call-done = bf16[2048,1024]{1,0:T(8,128)(2,1)} async-done(((bf16[16,1024]{1,0:T(8,128)(2,1)}), bf16[2048,1024]{1,0:T(8,128)(2,1)}) %all-gather.6.cloned.1.call-update) | async-done | bytes 4194320 | tf_op jit(solution)/shard_map/all_gather | solution.py:84
  308.3 3.8 fusion.62
  312.1 127.1 %all-gather.8.cloned.1.call-done = bf16[2048,1024]{1,0:T(8,128)(2,1)} async-done(((bf16[16,1024]{1,0:T(8,128)(2,1)}), bf16[2048,1024]{1,0:T(8,128)(2,1)}) %all-gather.8.cloned.1.call-update) | async-done | bytes 4194320 | tf_op jit(solution)/shard_map/all_gather | solution.py:85
  439.1 7.1 %convolution_convert_fusion = bf16[256,2048]{0,1:T(8,128)(2,1)} fusion(bf16[1024,2048]{0,1:T(8,128)(2,1)} %bitcast.12, bf16[256,2048]{0,1:T(8,128)(2,1)S(1)} %copy-done.3, bf16[2048,1024]{1,0:T(8,128)(2,1)} %all-gather.8.cloned.1.call-done, f32[256,1024]{1,0:T(8,128)S(1)} %fusion.62), kind=kOutput, calls=%fused_computation | convolution fusion | flops 2149580800 | bytes 11534336 | tf_op jit(solution)/shard_map/dot_general | solution.py:94
  447.1 50.4 %all-reduce.2.cloned.1.call-done = bf16[256,2048]{0,1:T(8,128)(2,1)} async-done(((bf16[256,2048]{0,1:T(8,128)(2,1)}), bf16[256,2048]{0,1:T(8,128)(2,1)}) %all-reduce.2.cloned.1.call-update) | async-done | bytes 1048592 | tf_op jit(solution)/shard_map/psum | solution.py:96
  497.5 1.0 convert_add_fusion
  (49 shorter events, 9.3 us)
Async XLA Ops:
  7.2 38.1 %copy-start.4 = (bf16[256,512]{1,0:T(8,128)(2,1)S(1)}, bf16[256,512]{1,0:T(8,128)(2,1)}, u32[]{:S(2)}) copy-start(bf16[256,512]{1,0:T(8,128)(2,1)} %param.12) | copy-start | bytes 786436
  7.2 138.8 %all-gather.4.cloned.1.call-start = ((), (), s32[]{:S(2)}) async-start(), calls=%async_computation.1 | async-start | bytes 1310720 | tf_op jit(solution)/shard_map/all_gather | solution.py:82
  9.9 26.4 %collective-permute-start = (bf16[256]{0:T(256)(128)(2,1)S(1)}, bf16[256]{0:T(256)(128)(2,1)S(1)}, u32[]{:S(2)}, u32[]{:S(2)}) collective-permute-start(bf16[256]{0:T(256)(128)(2,1)S(1)} %get-tuple-element.23), channel_id=1, source_target_pairs={{0,8},{4,12},{8,16},{12,20},{16,24},{20,28},{24,32},{28,36},{32,40... | collective-permute-start | bytes 1544 | tf_op jit(solution)/shard_map/ppermute | solution.py:17
  18.2 22.3 %collective-permute-start.1 = (bf16[256]{0:T(256)(128)(2,1)S(1)}, bf16[256]{0:T(256)(128)(2,1)S(1)}, u32[]{:S(2)}, u32[]{:S(2)}) collective-permute-start(bf16[256]{0:T(256)(128)(2,1)S(1)} %get-tuple-element.23), channel_id=1, source_target_pairs={{0,4},{4,8},{8,12},{12,16},{16,20},{20,24},{24,28},{28,32},{32,36}... | collective-permute-start | bytes 1544 | tf_op jit(solution)/shard_map/ppermute | solution.py:17
  20.6 19.9 %collective-permute-start.2 = (bf16[256,512]{1,0:T(8,128)(2,1)}, bf16[256,512]{1,0:T(8,128)(2,1)S(1)}, u32[]{:S(2)}, u32[]{:S(2)}) collective-permute-start(bf16[256,512]{1,0:T(8,128)(2,1)} %param.13), channel_id=1, source_target_pairs={{0,8},{4,12},{8,16},{12,20},{16,24},{20,28},{24,32},{28,36},{32,40... | collective-permute-start | bytes 786440 | tf_op jit(solution)/shard_map/ppermute | solution.py:17
  26.0 17.0 %collective-permute-start.3 = (bf16[256,512]{1,0:T(8,128)(2,1)}, bf16[256,512]{1,0:T(8,128)(2,1)S(1)}, u32[]{:S(2)}, u32[]{:S(2)}) collective-permute-start(bf16[256,512]{1,0:T(8,128)(2,1)} %param.13), channel_id=1, source_target_pairs={{0,4},{4,8},{8,12},{12,16},{16,20},{20,24},{24,28},{28,32},{32,36}... | collective-permute-start | bytes 786440 | tf_op jit(solution)/shard_map/ppermute | solution.py:17
  31.4 17.8 %collective-permute-start.4 = (bf16[256,512]{1,0:T(8,128)(2,1)}, bf16[256,512]{1,0:T(8,128)(2,1)S(1)}, u32[]{:S(2)}, u32[]{:S(2)}) collective-permute-start(bf16[256,512]{1,0:T(8,128)(2,1)} %param.14), channel_id=1, source_target_pairs={{0,8},{4,12},{8,16},{12,20},{16,24},{20,28},{24,32},{28,36},{32,40... | collective-permute-start | bytes 786440 | tf_op jit(solution)/shard_map/ppermute | solution.py:17
  36.3 23.5 %collective-permute-start.5 = (bf16[256,512]{1,0:T(8,128)(2,1)}, bf16[256,512]{1,0:T(8,128)(2,1)S(1)}, u32[]{:S(2)}, u32[]{:S(2)}) collective-permute-start(bf16[256,512]{1,0:T(8,128)(2,1)} %param.14), channel_id=1, source_target_pairs={{0,4},{4,8},{8,12},{12,16},{16,20},{20,24},{24,28},{28,32},{32,36}... | collective-permute-start | bytes 786440 | tf_op jit(solution)/shard_map/ppermute | solution.py:17
  43.9 15.9 %copy-start = (bf16[256,512]{1,0:T(8,128)(2,1)S(1)}, bf16[256,512]{1,0:T(8,128)(2,1)}, u32[]{:S(2)}) copy-start(bf16[256,512]{1,0:T(8,128)(2,1)} %param.14) | copy-start | bytes 786436
  61.5 19.3 %copy-start.2 = (f32[512]{0:T(512)S(1)}, f32[512]{0:T(512)}, u32[]{:S(2)}) copy-start(f32[512]{0:T(512)} %param.16) | copy-start | bytes 6148
  62.1 21.0 %copy-start.1 = (bf16[1024,16]{0,1:T(8,128)(2,1)S(1)}, bf16[1024,16]{0,1:T(8,128)(2,1)}, u32[]{:S(2)}) copy-start(bf16[1024,16]{0,1:T(8,128)(2,1)} %param.19) | copy-start | bytes 98308
  81.6 226.6 %all-gather.6.cloned.1.call-start = ((), (), s32[]{:S(2)}) async-start(), calls=%async_computation.2 | async-start | bytes 4227072 | tf_op jit(solution)/shard_map/all_gather | solution.py:84
  82.4 356.7 %all-gather.8.cloned.1.call-start = ((), (), s32[]{:S(2)}) async-start(), calls=%async_computation.3 | async-start | bytes 4227072 | tf_op jit(solution)/shard_map/all_gather | solution.py:85
  85.6 353.5 %all-to-all-start = ((bf16[128,1024,16]{1,2,0:T(8,128)(2,1)}), bf16[128,1024,16]{1,2,0:T(8,128)(2,1)}, u32[]{:S(2)}, u32[]{:S(2)}) async-start(bf16[128,1024,16]{1,2,0:T(8,128)(2,1)} %stack.2), calls=%async_computation | async-start | bytes 8388608 | tf_op jit(solution)/shard_map/all_to_all | solution.py:92
  105.6 391.9 %all-reduce.2.cloned.1.call-start = ((), (), s32[]{:S(2)}) async-start(), calls=%async_computation.4 | async-start | bytes 2097152 | tf_op jit(solution)/shard_map/psum | solution.py:96
  146.0 293.1 %copy-start.3 = (bf16[256,2048]{0,1:T(8,128)(2,1)S(1)}, bf16[256,2048]{0,1:T(8,128)(2,1)}, u32[]{:S(2)}) copy-start(bf16[256,2048]{0,1:T(8,128)(2,1)} %all-gather.4.cloned.1.call-done) | copy-start | bytes 3145732
Sparse Core Ops, SparseCore 0:
  81.8 64.2 all-gather.3
  150.5 157.6 all-gather.5
  312.8 126.2 all-gather.7
  446.4 51.0 all-reduce.1
